TPU v7x, 512 devices: a whole 4x4x16 slice. The times are simulated.
512 devices in a mesh: mx: 16 (over y, z_hi), my: 16 (over x, z_lo), dz: 2 (over core).
Axes of the slice: x: 4, y: 4, z: 16 (z_hi: 4, z_lo: 4; z = z_hi * 4 + z_lo), core: 2. Of those that a mesh axis runs over, the one named last changes fastest.
Arguments:
- electric: float32 [3, 16, 256, 2048], P(None, 'dz', 'mx', 'my'), may hold values from -6 to 6
- magnetic: float32 [3, 16, 256, 2048], P(None, 'dz', 'mx', 'my'), may hold values from -6 to 6
- poles: float32 [3, 3, 16, 256, 2048], P(None, None, 'dz', 'mx', 'my'), may hold values from -4 to 4
- material: int32 [16, 256, 2048], P('dz', 'mx', 'my'), may hold values from 0 to 3
- exit_layer: int32 [1], replicated, may hold values from 0 to 15
Outputs:
- electric_next: float32 [3, 16, 256, 2048], P(None, 'dz', 'mx', 'my')
- magnetic_next: float32 [3, 16, 256, 2048], P(None, 'dz', 'mx', 'my')
- poles_next: float32 [3, 3, 16, 256, 2048], P(None, None, 'dz', 'mx', 'my')
- far_field: float32 [4, 2, 2, 128, 128], P('dz', None, None, 'mx', 'my')
All inputs are finite; a program needn't handle non-finite values.
Results may differ from a plain program's by a relative error of at most 0.00016.
Values sent between devices are 32-bit elements; how exact they have to be, the bound alone decides.
A program may use at most 64 MiB of HBM per device.

v0:
```python
import math
import jax
import jax.numpy as jnp
import numpy as np
from jax import lax
from jax.sharding import PartitionSpec as P

STEPS = 4
W = 4
U = 128
V = 128
time_step = 0.5
eps_inf = np.array([1.0, 4.0, 2.1, 1.5])
drude_plasma = np.array([0.0, 0.0, 0.0, 2.0])
drude_damping = np.array([0.0, 0.0, 0.0, 0.1])
lorentz_square = np.array([0.3, 0.8, 1.0, 0.5])
lorentz_strength = np.array([0.0, 1.5, 0.1, 0.8])
lorentz_damping = np.array([0.0, 0.05, 0.02, 0.2])
drude_keep = (1.0 - drude_damping * time_step / 2) / (1.0 + drude_damping * time_step / 2)
drude_drive = drude_plasma * time_step / (1.0 + drude_damping * time_step / 2)
lorentz_keep = (1.0 - lorentz_damping * time_step / 2) / (1.0 + lorentz_damping * time_step / 2)
lorentz_push = time_step / (1.0 + lorentz_damping * time_step / 2)
coef_table = np.stack(
    [
        drude_keep,
        drude_drive,
        lorentz_keep,
        lorentz_push * lorentz_square * lorentz_strength,
        lorentz_push * lorentz_square,
        time_step / eps_inf,
    ]
).astype(np.float32)


def from_behind(x, axis, by):
    devices = lax.axis_size(axis)
    pairs = [(i, i + by) for i in range(devices) if 0 <= i + by < devices]
    return lax.ppermute(x, axis, pairs)


def coefficients(material):
    result = []
    for row in range(6):
        value = jnp.zeros(material.shape, jnp.float32)
        for which in range(4):
            value = value + jnp.where(
                material == which, jnp.float32(coef_table[row, which]), jnp.float32(0.0)
            )
        result.append(value)
    return result


def first_layer(field, axis):
    return lax.slice_in_dim(field, 0, 1, axis=axis)


def last_layer(field, axis):
    return lax.slice_in_dim(field, field.shape[axis] - 1, field.shape[axis], axis=axis)


def rim_forward(field, rim, axis):
    inner = lax.slice_in_dim(field, 1, field.shape[axis], axis=axis)
    return jnp.concatenate([inner, rim], axis) - field


def rim_backward(field, rim, axis):
    inner = lax.slice_in_dim(field, 0, field.shape[axis] - 1, axis=axis)
    return field - jnp.concatenate([rim, inner], axis)


def curl_electric(electric):
    part_x, part_y, part_z = (electric[0], electric[1], electric[2])
    xrim_y, xrim_z = from_behind((first_layer(part_y, 1), first_layer(part_z, 1)), "mx", -1)
    yrim_x, yrim_z = from_behind((first_layer(part_x, 2), first_layer(part_z, 2)), "my", -1)
    zrim_x, zrim_y = from_behind((first_layer(part_x, 0), first_layer(part_y, 0)), "dz", -1)
    return jnp.stack(
        [
            rim_forward(part_z, yrim_z, 2) - rim_forward(part_y, zrim_y, 0),
            rim_forward(part_x, zrim_x, 0) - rim_forward(part_z, xrim_z, 1),
            rim_forward(part_y, xrim_y, 1) - rim_forward(part_x, yrim_x, 2),
        ]
    )


def curl_magnetic(magnetic):
    part_x, part_y, part_z = (magnetic[0], magnetic[1], magnetic[2])
    xrim_y, xrim_z = from_behind((last_layer(part_y, 1), last_layer(part_z, 1)), "mx", 1)
    yrim_x, yrim_z = from_behind((last_layer(part_x, 2), last_layer(part_z, 2)), "my", 1)
    zrim_x, zrim_y = from_behind((last_layer(part_x, 0), last_layer(part_y, 0)), "dz", 1)
    return jnp.stack(
        [
            rim_backward(part_z, yrim_z, 2) - rim_backward(part_y, zrim_y, 0),
            rim_backward(part_x, zrim_x, 0) - rim_backward(part_z, xrim_z, 1),
            rim_backward(part_y, xrim_y, 1) - rim_backward(part_x, yrim_x, 2),
        ]
    )


def phase_tables(waves, total_steps):
    period = (8 + 2 * waves).astype(jnp.float32)
    moments = jnp.arange(1, total_steps + 1).astype(jnp.float32)
    angle = 2 * math.pi * moments[None, :] / period[:, None]
    return (jnp.cos(angle), jnp.sin(angle))


def transform_table(waves, outputs, positions, center, scale):
    rows = jnp.arange(outputs) - outputs // 2
    product = rows[:, None] * (positions - center)[None, :]
    period = outputs * (5 + waves)
    folded = jnp.mod(product[None, :, :], period[:, None, None])
    angle = 2 * math.pi * folded.astype(jnp.float32) / period.astype(jnp.float32)[:, None, None]
    return (scale * jnp.cos(angle), -scale * jnp.sin(angle))


def product_of(form, left, right):
    return jnp.einsum(form, left, right, precision=lax.Precision.HIGHEST)


def along_rows(kern_re, kern_im, data_re, data_im):
    form = "wux,wpxy->wpuy"
    real = product_of(form, kern_re, data_re) - product_of(form, kern_im, data_im)
    imag = product_of(form, kern_re, data_im) + product_of(form, kern_im, data_re)
    return (real, imag)


def along_columns(data_re, data_im, kern_re, kern_im):
    form = "wpuy,wvy->wpuv"
    real = product_of(form, data_re, kern_re) - product_of(form, data_im, kern_im)
    imag = product_of(form, data_im, kern_re) + product_of(form, data_re, kern_im)
    return (real, imag)


def body(electric, magnetic, poles, material, exit_layer):
    depth, cells_x, cells_y = material.shape
    keep_d, drive_d, keep_l, drive_l, restore_l, scale_e = coefficients(material)
    depth_index = lax.axis_index("dz") * depth + jnp.arange(depth)
    selector = (depth_index == exit_layer[0]).astype(jnp.float32)
    polar, current, drude = (poles[0], poles[1], poles[2])
    planes = []
    for _ in range(STEPS):
        magnetic = magnetic - time_step * curl_electric(electric)
        current_new = keep_l * current + drive_l * electric - restore_l * polar
        polar = polar + time_step * current_new
        drude_new = keep_d * drude + drive_d * electric
        electric = electric + scale_e * (
            curl_magnetic(magnetic) - 0.5 * (drude + drude_new) - current_new
        )
        current, drude = (current_new, drude_new)
        planes.append(product_of("z,czxy->cxy", selector, electric[:2]))
    planes = jnp.stack(planes)
    cos_t, sin_t = phase_tables(jnp.arange(W), STEPS)
    phasor = jnp.stack(
        [product_of("wn,npxy->wpxy", cos_t, planes), -product_of("wn,npxy->wpxy", sin_t, planes)], 1
    )
    mine = lax.psum_scatter(phasor, "dz", scatter_dimension=0, tiled=True)
    local_waves = mine.shape[0]
    waves = lax.axis_index("dz") * local_waves + jnp.arange(local_waves).astype(jnp.int32)
    total_x = cells_x * lax.axis_size("mx")
    total_y = cells_y * lax.axis_size("my")
    pos_x = lax.axis_index("mx") * cells_x + jnp.arange(cells_x)
    pos_y = lax.axis_index("my") * cells_y + jnp.arange(cells_y)
    row_re, row_im = transform_table(waves, U, pos_x, total_x // 2, 1.0 / math.sqrt(total_x))
    col_re, col_im = transform_table(waves, V, pos_y, total_y // 2, 1.0 / math.sqrt(total_y))
    mid_re, mid_im = along_rows(row_re, row_im, mine[:, 0], mine[:, 1])
    rows_share = U // lax.axis_size("mx")
    cols_share = V // lax.axis_size("my")
    far_re, far_im = along_columns(mid_re, mid_im, col_re, col_im)
    total = lax.psum(jnp.stack([far_re, far_im], 1), ("mx", "my"))
    total = lax.dynamic_slice_in_dim(total, lax.axis_index("mx") * rows_share, rows_share, 3)
    far_field = lax.dynamic_slice_in_dim(total, lax.axis_index("my") * cols_share, cols_share, 4)
    poles_next = jnp.stack([polar, current, drude])
    return (electric, magnetic, poles_next, far_field)


def solution(mesh):
    return jax.shard_map(
        body,
        mesh=mesh,
        in_specs=(
            P(None, "dz", "mx", "my"),
            P(None, "dz", "mx", "my"),
            P(None, None, "dz", "mx", "my"),
            P("dz", "mx", "my"),
            P(),
        ),
        out_specs=(
            P(None, "dz", "mx", "my"),
            P(None, "dz", "mx", "my"),
            P(None, None, "dz", "mx", "my"),
            P("dz", None, None, "mx", "my"),
        ),
        check_vma=False,
    )
```

profile of v0, /device:TPU:4, one launch (start us, length us, event | category | flops | bytes accessed | tf_op | source)
XLA Modules:
  0.0 669.9 jit_solution(14490689699884551274)
XLA Ops:
  8.2 6.5 collective-permute-start
  25.4 4.0 collective-permute-done.4
  30.5 3.8 collective-permute-start.6
  34.3 7.8 %collective-permute-start.9 = (f32[8,1,128]{2,1,0:T(1,128)S(1)}, f32[8,1,128]{2,1,0:T(1,128)S(1)}, u32[]{:S(2)}, u32[]{:S(2)}) collective-permute-start(f32[8,1,128]{2,1,0:T(1,128)S(1)} %slice.645), channel_id=1, source_target_pairs={{0,32},{32,64},{64,96},{96,128},{128,160},{160,192},{192,224},{224... | collective-permute-start | bytes 12296 | tf_op jit(solution)/shard_map/ppermute | solution.py:38
  47.8 7.8 %collective-permute-start.10 = (f32[8,1,128]{2,1,0:T(1,128)S(1)}, f32[8,1,128]{2,1,0:T(1,128)S(1)}, u32[]{:S(2)}, u32[]{:S(2)}) collective-permute-start(f32[8,1,128]{2,1,0:T(1,128)S(1)} %slice.647), channel_id=1, source_target_pairs={{0,32},{32,64},{64,96},{96,128},{128,160},{160,192},{192,224},{224... | collective-permute-start | bytes 12296 | tf_op jit(solution)/shard_map/ppermute | solution.py:38
  57.3 6.6 collective-permute-start.12
  68.1 5.5 collective-permute-done.15
  79.9 5.7 collective-permute-done.16
  85.9 3.4 collective-permute-start.18
  89.3 7.8 %collective-permute-start.21 = (f32[8,1,128]{2,1,0:T(1,128)S(1)}, f32[8,1,128]{2,1,0:T(1,128)S(1)}, u32[]{:S(2)}, u32[]{:S(2)}) collective-permute-start(f32[8,1,128]{2,1,0:T(1,128)S(1)} %slice.675), channel_id=1, source_target_pairs={{0,32},{32,64},{64,96},{96,128},{128,160},{160,192},{192,224},{224... | collective-permute-start | bytes 12296 | tf_op jit(solution)/shard_map/ppermute | solution.py:38
  102.7 7.3 %collective-permute-start.22 = (f32[8,1,128]{2,1,0:T(1,128)S(1)}, f32[8,1,128]{2,1,0:T(1,128)S(1)}, u32[]{:S(2)}, u32[]{:S(2)}) collective-permute-start(f32[8,1,128]{2,1,0:T(1,128)S(1)} %slice.677), channel_id=1, source_target_pairs={{0,32},{32,64},{64,96},{96,128},{128,160},{160,192},{192,224},{224... | collective-permute-start | bytes 12296 | tf_op jit(solution)/shard_map/ppermute | solution.py:38
  111.6 6.6 collective-permute-start.24
  122.5 6.0 collective-permute-done.27
  128.6 3.0 collective-permute-start.29
  134.8 6.5 collective-permute-done.28
  144.5 7.8 %collective-permute-start.33 = (f32[8,1,128]{2,1,0:T(1,128)S(1)}, f32[8,1,128]{2,1,0:T(1,128)S(1)}, u32[]{:S(2)}, u32[]{:S(2)}) collective-permute-start(f32[8,1,128]{2,1,0:T(1,128)S(1)} %slice.705), channel_id=1, source_target_pairs={{0,32},{32,64},{64,96},{96,128},{128,160},{160,192},{192,224},{224... | collective-permute-start | bytes 12296 | tf_op jit(solution)/shard_map/ppermute | solution.py:38
  157.9 7.8 %collective-permute-start.34 = (f32[8,1,128]{2,1,0:T(1,128)S(1)}, f32[8,1,128]{2,1,0:T(1,128)S(1)}, u32[]{:S(2)}, u32[]{:S(2)}) collective-permute-start(f32[8,1,128]{2,1,0:T(1,128)S(1)} %slice.707), channel_id=1, source_target_pairs={{0,32},{32,64},{64,96},{96,128},{128,160},{160,192},{192,224},{224... | collective-permute-start | bytes 12296 | tf_op jit(solution)/shard_map/ppermute | solution.py:38
  167.4 6.6 collective-permute-start.36
  178.3 5.5 collective-permute-done.39
  190.1 6.2 collective-permute-done.40
  199.5 7.8 %collective-permute-start.45 = (f32[8,1,128]{2,1,0:T(1,128)S(1)}, f32[8,1,128]{2,1,0:T(1,128)S(1)}, u32[]{:S(2)}, u32[]{:S(2)}) collective-permute-start(f32[8,1,128]{2,1,0:T(1,128)S(1)} %slice.735), channel_id=1, source_target_pairs={{0,32},{32,64},{64,96},{96,128},{128,160},{160,192},{192,224},{224... | collective-permute-start | bytes 12296 | tf_op jit(solution)/shard_map/ppermute | solution.py:38
  212.9 7.8 %collective-permute-start.46 = (f32[8,1,128]{2,1,0:T(1,128)S(1)}, f32[8,1,128]{2,1,0:T(1,128)S(1)}, u32[]{:S(2)}, u32[]{:S(2)}) collective-permute-start(f32[8,1,128]{2,1,0:T(1,128)S(1)} %slice.737), channel_id=1, source_target_pairs={{0,32},{32,64},{64,96},{96,128},{128,160},{160,192},{192,224},{224... | collective-permute-start | bytes 12296 | tf_op jit(solution)/shard_map/ppermute | solution.py:38
  224.9 23.1 %reduce-scatter.2.cloned.1.call-done = f32[2,2,2,16,128]{4,3,2,1,0:T(8,128)} async-done(((f32[4,2,2,16,128]{4,3,2,1,0:T(8,128)}), f32[2,2,2,16,128]{4,3,2,1,0:T(8,128)}) %reduce-scatter.2.cloned.1.call-update) | async-done | bytes 65552 | tf_op jit(solution)/shard_map/reduce_scatter | solution.py:155
  262.3 399.2 %all-reduce.2.cloned.1.call-done = f32[2,2,2,128,128]{4,3,2,0,1:T(8,128)} async-done(((f32[2,2,2,128,128]{4,3,2,0,1:T(8,128)}), f32[2,2,2,128,128]{4,3,2,0,1:T(8,128)}) %all-reduce.2.cloned.1.call-update) | async-done | bytes 524304 | tf_op jit(solution)/shard_map/psum | solution.py:168
  (228 shorter events, 93.5 us)
Async XLA Ops:
  7.2 240.8 %reduce-scatter.2.cloned.1.call-start = ((), (), s32[]{:S(2)}) async-start(), calls=%async_computation.1 | async-start | bytes 196608 | tf_op jit(solution)/shard_map/reduce_scatter | solution.py:155
  8.2 14.4 %collective-permute-start = (f32[8,16,1]{2,1,0:T(8,128)S(1)}, f32[8,16,1]{2,1,0:T(8,128)S(1)}, u32[]{:S(2)}, u32[]{:S(2)}) collective-permute-start(f32[8,16,1]{2,1,0:T(8,128)S(1)} %bitcast.384), channel_id=1, source_target_pairs={{2,0},{4,2},{6,4},{8,6},{10,8},{12,10},{14,12},{16,14},{18,16},{20... | collective-permute-start | bytes 1544 | tf_op jit(solution)/shard_map/ppermute | solution.py:38
  14.7 10.7 %collective-permute-start.3 = (f32[8,1,128]{2,1,0:T(1,128)S(1)}, f32[8,1,128]{2,1,0:T(1,128)S(1)}, u32[]{:S(2)}, u32[]{:S(2)}) collective-permute-start(f32[8,1,128]{2,1,0:T(1,128)S(1)} %slice.631), channel_id=1, source_target_pairs={{32,0},{64,32},{96,64},{128,96},{160,128},{192,160},{224,192},{256... | collective-permute-start | bytes 12296 | tf_op jit(solution)/shard_map/ppermute | solution.py:38
  18.0 11.3 %collective-permute-start.4 = (f32[8,1,128]{2,1,0:T(1,128)S(1)}, f32[8,1,128]{2,1,0:T(1,128)S(1)}, u32[]{:S(2)}, u32[]{:S(2)}) collective-permute-start(f32[8,1,128]{2,1,0:T(1,128)S(1)} %slice.633), channel_id=1, source_target_pairs={{32,0},{64,32},{96,64},{128,96},{160,128},{192,160},{224,192},{256... | collective-permute-start | bytes 12296 | tf_op jit(solution)/shard_map/ppermute | solution.py:38
  19.4 10.0 %collective-permute-start.1 = (f32[1,16,128]{2,1,0:T(8,128)S(1)}, f32[1,16,128]{2,1,0:T(8,128)S(1)}, u32[]{:S(2)}, u32[]{:S(2)}) collective-permute-start(f32[1,16,128]{2,1,0:T(8,128)S(1)} %get-tuple-element.102), channel_id=1, source_target_pairs={{1,0},{3,2},{5,4},{7,6},{9,8},{11,10},{13,12},{15,14},{17,16},{19,... | collective-permute-start | bytes 24584 | tf_op jit(solution)/shard_map/ppermute | solution.py:38
  30.5 14.3 %collective-permute-start.6 = (f32[8,16,1]{2,1,0:T(8,128)S(1)}, f32[8,16,1]{2,1,0:T(8,128)S(1)}, u32[]{:S(2)}, u32[]{:S(2)}) collective-permute-start(f32[8,16,1]{2,1,0:T(8,128)S(1)} %slice.637), channel_id=1, source_target_pairs={{0,2},{2,4},{4,6},{6,8},{8,10},{10,12},{12,14},{14,16},{16,18},{18... | collective-permute-start | bytes 1544 | tf_op jit(solution)/shard_map/ppermute | solution.py:38
  34.3 10.5 %collective-permute-start.9 = (f32[8,1,128]{2,1,0:T(1,128)S(1)}, f32[8,1,128]{2,1,0:T(1,128)S(1)}, u32[]{:S(2)}, u32[]{:S(2)}) collective-permute-start(f32[8,1,128]{2,1,0:T(1,128)S(1)} %slice.645), channel_id=1, source_target_pairs={{0,32},{32,64},{64,96},{96,128},{128,160},{160,192},{192,224},{224... | collective-permute-start | bytes 12296 | tf_op jit(solution)/shard_map/ppermute | solution.py:38
  45.7 9.9 %collective-permute-start.11 = (f32[8,16,1]{2,1,0:T(8,128)S(1)}, f32[8,16,1]{2,1,0:T(8,128)S(1)}, u32[]{:S(2)}, u32[]{:S(2)}) collective-permute-start(f32[8,16,1]{2,1,0:T(8,128)S(1)} %slice.649), channel_id=1, source_target_pairs={{0,2},{2,4},{4,6},{6,8},{8,10},{10,12},{12,14},{14,16},{16,18},{18... | collective-permute-start | bytes 1544 | tf_op jit(solution)/shard_map/ppermute | solution.py:38
  57.3 10.8 %collective-permute-start.12 = (f32[8,16,1]{2,1,0:T(8,128)S(1)}, f32[8,16,1]{2,1,0:T(8,128)S(1)}, u32[]{:S(2)}, u32[]{:S(2)}) collective-permute-start(f32[8,16,1]{2,1,0:T(8,128)S(1)} %bitcast.381), channel_id=1, source_target_pairs={{2,0},{4,2},{6,4},{8,6},{10,8},{12,10},{14,12},{16,14},{18,16},{20... | collective-permute-start | bytes 1544 | tf_op jit(solution)/shard_map/ppermute | solution.py:38
  63.9 9.7 %collective-permute-start.15 = (f32[8,1,128]{2,1,0:T(1,128)S(1)}, f32[8,1,128]{2,1,0:T(1,128)S(1)}, u32[]{:S(2)}, u32[]{:S(2)}) collective-permute-start(f32[8,1,128]{2,1,0:T(1,128)S(1)} %slice.661), channel_id=1, source_target_pairs={{32,0},{64,32},{96,64},{128,96},{160,128},{192,160},{224,192},{256... | collective-permute-start | bytes 12296 | tf_op jit(solution)/shard_map/ppermute | solution.py:38
  75.9 9.7 %collective-permute-start.16 = (f32[8,1,128]{2,1,0:T(1,128)S(1)}, f32[8,1,128]{2,1,0:T(1,128)S(1)}, u32[]{:S(2)}, u32[]{:S(2)}) collective-permute-start(f32[8,1,128]{2,1,0:T(1,128)S(1)} %slice.663), channel_id=1, source_target_pairs={{32,0},{64,32},{96,64},{128,96},{160,128},{192,160},{224,192},{256... | collective-permute-start | bytes 12296 | tf_op jit(solution)/shard_map/ppermute | solution.py:38
  85.9 13.9 %collective-permute-start.18 = (f32[8,16,1]{2,1,0:T(8,128)S(1)}, f32[8,16,1]{2,1,0:T(8,128)S(1)}, u32[]{:S(2)}, u32[]{:S(2)}) collective-permute-start(f32[8,16,1]{2,1,0:T(8,128)S(1)} %slice.667), channel_id=1, source_target_pairs={{0,2},{2,4},{4,6},{6,8},{8,10},{10,12},{12,14},{14,16},{16,18},{18... | collective-permute-start | bytes 1544 | tf_op jit(solution)/shard_map/ppermute | solution.py:38
  89.3 10.5 %collective-permute-start.21 = (f32[8,1,128]{2,1,0:T(1,128)S(1)}, f32[8,1,128]{2,1,0:T(1,128)S(1)}, u32[]{:S(2)}, u32[]{:S(2)}) collective-permute-start(f32[8,1,128]{2,1,0:T(1,128)S(1)} %slice.675), channel_id=1, source_target_pairs={{0,32},{32,64},{64,96},{96,128},{128,160},{160,192},{192,224},{224... | collective-permute-start | bytes 12296 | tf_op jit(solution)/shard_map/ppermute | solution.py:38
  111.6 10.8 %collective-permute-start.24 = (f32[8,16,1]{2,1,0:T(8,128)S(1)}, f32[8,16,1]{2,1,0:T(8,128)S(1)}, u32[]{:S(2)}, u32[]{:S(2)}) collective-permute-start(f32[8,16,1]{2,1,0:T(8,128)S(1)} %bitcast.382), channel_id=1, source_target_pairs={{2,0},{4,2},{6,4},{8,6},{10,8},{12,10},{14,12},{16,14},{18,16},{20... | collective-permute-start | bytes 1544 | tf_op jit(solution)/shard_map/ppermute | solution.py:38
  118.2 10.2 %collective-permute-start.27 = (f32[8,1,128]{2,1,0:T(1,128)S(1)}, f32[8,1,128]{2,1,0:T(1,128)S(1)}, u32[]{:S(2)}, u32[]{:S(2)}) collective-permute-start(f32[8,1,128]{2,1,0:T(1,128)S(1)} %slice.691), channel_id=1, source_target_pairs={{32,0},{64,32},{96,64},{128,96},{160,128},{192,160},{224,192},{256... | collective-permute-start | bytes 12296 | tf_op jit(solution)/shard_map/ppermute | solution.py:38
  131.6 9.7 %collective-permute-start.28 = (f32[8,1,128]{2,1,0:T(1,128)S(1)}, f32[8,1,128]{2,1,0:T(1,128)S(1)}, u32[]{:S(2)}, u32[]{:S(2)}) collective-permute-start(f32[8,1,128]{2,1,0:T(1,128)S(1)} %slice.693), channel_id=1, source_target_pairs={{32,0},{64,32},{96,64},{128,96},{160,128},{192,160},{224,192},{256... | collective-permute-start | bytes 12296 | tf_op jit(solution)/shard_map/ppermute | solution.py:38
  141.6 13.3 %collective-permute-start.30 = (f32[8,16,1]{2,1,0:T(8,128)S(1)}, f32[8,16,1]{2,1,0:T(8,128)S(1)}, u32[]{:S(2)}, u32[]{:S(2)}) collective-permute-start(f32[8,16,1]{2,1,0:T(8,128)S(1)} %slice.697), channel_id=1, source_target_pairs={{0,2},{2,4},{4,6},{6,8},{8,10},{10,12},{12,14},{14,16},{16,18},{18... | collective-permute-start | bytes 1544 | tf_op jit(solution)/shard_map/ppermute | solution.py:38
  144.5 10.5 %collective-permute-start.33 = (f32[8,1,128]{2,1,0:T(1,128)S(1)}, f32[8,1,128]{2,1,0:T(1,128)S(1)}, u32[]{:S(2)}, u32[]{:S(2)}) collective-permute-start(f32[8,1,128]{2,1,0:T(1,128)S(1)} %slice.705), channel_id=1, source_target_pairs={{0,32},{32,64},{64,96},{96,128},{128,160},{160,192},{192,224},{224... | collective-permute-start | bytes 12296 | tf_op jit(solution)/shard_map/ppermute | solution.py:38
  155.9 9.8 %collective-permute-start.35 = (f32[8,16,1]{2,1,0:T(8,128)S(1)}, f32[8,16,1]{2,1,0:T(8,128)S(1)}, u32[]{:S(2)}, u32[]{:S(2)}) collective-permute-start(f32[8,16,1]{2,1,0:T(8,128)S(1)} %slice.709), channel_id=1, source_target_pairs={{0,2},{2,4},{4,6},{6,8},{8,10},{10,12},{12,14},{14,16},{16,18},{18... | collective-permute-start | bytes 1544 | tf_op jit(solution)/shard_map/ppermute | solution.py:38
  167.4 10.8 %collective-permute-start.36 = (f32[8,16,1]{2,1,0:T(8,128)S(1)}, f32[8,16,1]{2,1,0:T(8,128)S(1)}, u32[]{:S(2)}, u32[]{:S(2)}) collective-permute-start(f32[8,16,1]{2,1,0:T(8,128)S(1)} %bitcast.383), channel_id=1, source_target_pairs={{2,0},{4,2},{6,4},{8,6},{10,8},{12,10},{14,12},{16,14},{18,16},{20... | collective-permute-start | bytes 1544 | tf_op jit(solution)/shard_map/ppermute | solution.py:38
  196.6 13.3 %collective-permute-start.42 = (f32[8,16,1]{2,1,0:T(8,128)S(1)}, f32[8,16,1]{2,1,0:T(8,128)S(1)}, u32[]{:S(2)}, u32[]{:S(2)}) collective-permute-start(f32[8,16,1]{2,1,0:T(8,128)S(1)} %slice.727), channel_id=1, source_target_pairs={{0,2},{2,4},{4,6},{6,8},{8,10},{10,12},{12,14},{14,16},{16,18},{18... | collective-permute-start | bytes 1544 | tf_op jit(solution)/shard_map/ppermute | solution.py:38
  199.5 10.5 %collective-permute-start.45 = (f32[8,1,128]{2,1,0:T(1,128)S(1)}, f32[8,1,128]{2,1,0:T(1,128)S(1)}, u32[]{:S(2)}, u32[]{:S(2)}) collective-permute-start(f32[8,1,128]{2,1,0:T(1,128)S(1)} %slice.735), channel_id=1, source_target_pairs={{0,32},{32,64},{64,96},{96,128},{128,160},{160,192},{192,224},{224... | collective-permute-start | bytes 12296 | tf_op jit(solution)/shard_map/ppermute | solution.py:38
  211.0 9.8 %collective-permute-start.47 = (f32[8,16,1]{2,1,0:T(8,128)S(1)}, f32[8,16,1]{2,1,0:T(8,128)S(1)}, u32[]{:S(2)}, u32[]{:S(2)}) collective-permute-start(f32[8,16,1]{2,1,0:T(8,128)S(1)} %slice.739), channel_id=1, source_target_pairs={{0,2},{2,4},{4,6},{6,8},{8,10},{10,12},{12,14},{14,16},{16,18},{18... | collective-permute-start | bytes 1544 | tf_op jit(solution)/shard_map/ppermute | solution.py:38
  224.6 437.0 %all-reduce.2.cloned.1.call-start = ((), (), s32[]{:S(2)}) async-start(), calls=%async_computation.2 | async-start | bytes 1048576 | tf_op jit(solution)/shard_map/psum | solution.py:168
  (33 other events, 217.1 us)
Sparse Core Ops, SparseCore 0:
  224.7 23.2 reduce-scatter.1
  261.5 399.9 all-reduce.1
where the time goes:
time: 671 us; the launch traced here: 670 us
  waiting for transfers between devices  478 us (71%)
  starting transfers between devices  151 us (23%)
  between operations  16.1 us (2%)
  matrix products  14.1 us (2%)
  local copies, waits for them, and re-layouts  6.84 us (1%)
    psum x1, waiting for transfers between devices, body(): total = lax.psum(jnp.stack([far_re, far_im], 1), ('mx', 'my'))  399 us
    ppermute x48, starting transfers between devices, from_behind(): return lax.ppermute(x, axis, pairs)  150 us
    ppermute x48, waiting for transfers between devices, from_behind(): return lax.ppermute(x, axis, pairs)  55.5 us
    reduce_scatter x1, waiting for transfers between devices, body(): mine = lax.psum_scatter(phasor, 'dz', scatter_dimension=0, tiled=True)  23.1 us
    dot_general x14, matrix products, product_of(): return jnp.einsum(form, left, right, precision=lax.Precision.HIGHEST)  14.1 us
  transfers between devices with their start and end apart: 50, of which 21 were waited for; matrix products, arithmetic and copies ran while one was open for 0% of the time, Pallas kernels for 0%

commit v1 on v0

--- a/solution.py
+++ b/solution.py
@@ -165,7 +165,9 @@
     rows_share = U // lax.axis_size("mx")
     cols_share = V // lax.axis_size("my")
     far_re, far_im = along_columns(mid_re, mid_im, col_re, col_im)
-    total = lax.psum(jnp.stack([far_re, far_im], 1), ("mx", "my"))
+    total = jnp.stack([far_re, far_im], 1)
+    for nth in ("mx", "my"):
+        total = jax.lax.psum(total, nth)
     total = lax.dynamic_slice_in_dim(total, lax.axis_index("mx") * rows_share, rows_share, 3)
     far_field = lax.dynamic_slice_in_dim(total, lax.axis_index("my") * cols_share, cols_share, 4)
     poles_next = jnp.stack([polar, current, drude])

time: 671 us -> 650 us (0.969)
  the two profiles are of different devices: /device:TPU:4 before, /device:TPU:8 now
where the time goes in v1:
time: 650 us; the launch traced here: 649 us
  waiting for transfers between devices  461 us (71%)
  starting transfers between devices  147 us (23%)
  between operations  15.8 us (2%)
  matrix products  14.1 us (2%)
  local copies, waits for them, and re-layouts  6.85 us (1%)
    psum x2, waiting for transfers between devices, body(): total = jax.lax.psum(total, nth)  378 us
    ppermute x48, starting transfers between devices, from_behind(): return lax.ppermute(x, axis, pairs)  146 us
    ppermute x48, waiting for transfers between devices, from_behind(): return lax.ppermute(x, axis, pairs)  66.7 us
    reduce_scatter x1, waiting for transfers between devices, body(): mine = lax.psum_scatter(phasor, 'dz', scatter_dimension=0, tiled=True)  16 us
    dot_general x14, matrix products, product_of(): return jnp.einsum(form, left, right, precision=lax.Precision.HIGHEST)  14.1 us
  transfers between devices with their start and end apart: 51, of which 21 were waited for; matrix products, arithmetic and copies ran while one was open for 0% of the time, Pallas kernels for 0%

profile of v1, /device:TPU:8, one launch (start us, length us, event | category | flops | bytes accessed | tf_op | source)
XLA Modules:
  0.0 648.9 jit_solution(13905828841242878273)
XLA Ops:
  9.5 12.6 %collective-permute-start.3 = (f32[8,1,128]{2,1,0:T(1,128)S(1)}, f32[8,1,128]{2,1,0:T(1,128)S(1)}, u32[]{:S(2)}, u32[]{:S(2)}) collective-permute-start(f32[8,1,128]{2,1,0:T(1,128)S(1)} %slice.631), channel_id=1, source_target_pairs={{32,0},{64,32},{96,64},{128,96},{160,128},{192,160},{224,192},{256... | collective-permute-start | bytes 12296 | tf_op jit(solution)/shard_map/ppermute | solution.py:38
  23.4 5.5 collective-permute-start.4
  36.3 5.2 collective-permute-start.6
  41.5 4.3 collective-permute-start.9
  52.0 4.1 collective-permute-start.11
  59.5 6.9 %collective-permute-done.10 = f32[8,1,128]{2,1,0:T(1,128)S(1)} collective-permute-done((f32[8,1,128]{2,1,0:T(1,128)S(1)}, f32[8,1,128]{2,1,0:T(1,128)S(1)}, u32[]{:S(2)}, u32[]{:S(2)}) %collective-permute-start.10) | collective-permute-done | bytes 4128 | tf_op jit(solution)/shard_map/ppermute | solution.py:38
  88.6 5.2 collective-permute-start.18
  93.8 4.7 collective-permute-start.21
  104.3 4.6 collective-permute-start.23
  112.8 6.5 collective-permute-done.22
  137.2 4.0 collective-permute-done.28
  141.6 5.1 collective-permute-start.30
  146.7 4.7 collective-permute-start.33
  157.2 6.6 %collective-permute-start.35 = (f32[8,16,1]{2,1,0:T(8,128)S(1)}, f32[8,16,1]{2,1,0:T(8,128)S(1)}, u32[]{:S(2)}, u32[]{:S(2)}) collective-permute-start(f32[8,16,1]{2,1,0:T(8,128)S(1)} %slice.709), channel_id=1, source_target_pairs={{0,2},{2,4},{4,6},{6,8},{8,10},{10,12},{12,14},{14,16},{16,18},{18... | collective-permute-start | bytes 1544 | tf_op jit(solution)/shard_map/ppermute | solution.py:38
  167.6 6.5 collective-permute-done.34
  186.7 4.0 collective-permute-start.40
  192.2 4.0 collective-permute-done.40
  196.6 5.1 collective-permute-start.42
  201.7 4.7 collective-permute-start.45
  212.2 6.6 %collective-permute-start.47 = (f32[8,16,1]{2,1,0:T(8,128)S(1)}, f32[8,16,1]{2,1,0:T(8,128)S(1)}, u32[]{:S(2)}, u32[]{:S(2)}) collective-permute-start(f32[8,16,1]{2,1,0:T(8,128)S(1)} %slice.739), channel_id=1, source_target_pairs={{0,2},{2,4},{4,6},{6,8},{8,10},{10,12},{12,14},{14,16},{16,18},{18... | collective-permute-start | bytes 1544 | tf_op jit(solution)/shard_map/ppermute | solution.py:38
  222.7 6.5 collective-permute-done.46
  232.0 16.0 %reduce-scatter.2.cloned.1.call-done = f32[2,2,2,16,128]{4,3,2,1,0:T(8,128)} async-done(((f32[4,2,2,16,128]{4,3,2,1,0:T(8,128)}), f32[2,2,2,16,128]{4,3,2,1,0:T(8,128)}) %reduce-scatter.2.cloned.1.call-update) | async-done | bytes 65552 | tf_op jit(solution)/shard_map/reduce_scatter | solution.py:155
  261.4 207.1 %all-reduce.3.cloned.1.call-done = f32[2,2,2,128,128]{4,3,2,0,1:T(8,128)} async-done(((f32[2,2,2,128,128]{4,3,2,0,1:T(8,128)}), f32[2,2,2,128,128]{4,3,2,0,1:T(8,128)}) %all-reduce.3.cloned.1.call-update) | async-done | bytes 524304 | tf_op jit(solution)/shard_map/psum | solution.py:170
  469.4 171.3 %all-reduce.5.cloned.1.call-done = f32[2,2,2,128,128]{4,3,2,0,1:T(8,128)} async-done(((f32[2,2,2,128,128]{4,3,2,0,1:T(8,128)}), f32[2,2,2,128,128]{4,3,2,0,1:T(8,128)}) %all-reduce.5.cloned.1.call-update) | async-done | bytes 524304 | tf_op jit(solution)/shard_map/psum | solution.py:170
  (231 shorter events, 121.4 us)
Async XLA Ops:
  7.2 240.8 %reduce-scatter.2.cloned.1.call-start = ((), (), s32[]{:S(2)}) async-start(), calls=%async_computation.1 | async-start | bytes 196608 | tf_op jit(solution)/shard_map/reduce_scatter | solution.py:155
  8.2 23.9 %collective-permute-start = (f32[8,16,1]{2,1,0:T(8,128)S(1)}, f32[8,16,1]{2,1,0:T(8,128)S(1)}, u32[]{:S(2)}, u32[]{:S(2)}) collective-permute-start(f32[8,16,1]{2,1,0:T(8,128)S(1)} %bitcast.384), channel_id=1, source_target_pairs={{2,0},{4,2},{6,4},{8,6},{10,8},{12,10},{14,12},{16,14},{18,16},{20... | collective-permute-start | bytes 1544 | tf_op jit(solution)/shard_map/ppermute | solution.py:38
  9.5 24.0 %collective-permute-start.3 = (f32[8,1,128]{2,1,0:T(1,128)S(1)}, f32[8,1,128]{2,1,0:T(1,128)S(1)}, u32[]{:S(2)}, u32[]{:S(2)}) collective-permute-start(f32[8,1,128]{2,1,0:T(1,128)S(1)} %slice.631), channel_id=1, source_target_pairs={{32,0},{64,32},{96,64},{128,96},{160,128},{192,160},{224,192},{256... | collective-permute-start | bytes 12296 | tf_op jit(solution)/shard_map/ppermute | solution.py:38
  22.1 11.3 %collective-permute-start.5 = (f32[8,16,1]{2,1,0:T(8,128)S(1)}, f32[8,16,1]{2,1,0:T(8,128)S(1)}, u32[]{:S(2)}, u32[]{:S(2)}) collective-permute-start(f32[8,16,1]{2,1,0:T(8,128)S(1)} %bitcast.388), channel_id=1, source_target_pairs={{2,0},{4,2},{6,4},{8,6},{10,8},{12,10},{14,12},{16,14},{18,16},{20... | collective-permute-start | bytes 1544 | tf_op jit(solution)/shard_map/ppermute | solution.py:38
  23.4 10.0 %collective-permute-start.4 = (f32[8,1,128]{2,1,0:T(1,128)S(1)}, f32[8,1,128]{2,1,0:T(1,128)S(1)}, u32[]{:S(2)}, u32[]{:S(2)}) collective-permute-start(f32[8,1,128]{2,1,0:T(1,128)S(1)} %slice.633), channel_id=1, source_target_pairs={{32,0},{64,32},{96,64},{128,96},{160,128},{192,160},{224,192},{256... | collective-permute-start | bytes 12296 | tf_op jit(solution)/shard_map/ppermute | solution.py:38
  36.3 12.3 %collective-permute-start.6 = (f32[8,16,1]{2,1,0:T(8,128)S(1)}, f32[8,16,1]{2,1,0:T(8,128)S(1)}, u32[]{:S(2)}, u32[]{:S(2)}) collective-permute-start(f32[8,16,1]{2,1,0:T(8,128)S(1)} %slice.637), channel_id=1, source_target_pairs={{0,2},{2,4},{4,6},{6,8},{8,10},{10,12},{12,14},{14,16},{16,18},{18... | collective-permute-start | bytes 1544 | tf_op jit(solution)/shard_map/ppermute | solution.py:38
  41.5 10.3 %collective-permute-start.9 = (f32[8,1,128]{2,1,0:T(1,128)S(1)}, f32[8,1,128]{2,1,0:T(1,128)S(1)}, u32[]{:S(2)}, u32[]{:S(2)}) collective-permute-start(f32[8,1,128]{2,1,0:T(1,128)S(1)} %slice.645), channel_id=1, source_target_pairs={{0,32},{32,64},{64,96},{96,128},{128,160},{160,192},{192,224},{224... | collective-permute-start | bytes 12296 | tf_op jit(solution)/shard_map/ppermute | solution.py:38
  56.1 10.3 %collective-permute-start.10 = (f32[8,1,128]{2,1,0:T(1,128)S(1)}, f32[8,1,128]{2,1,0:T(1,128)S(1)}, u32[]{:S(2)}, u32[]{:S(2)}) collective-permute-start(f32[8,1,128]{2,1,0:T(1,128)S(1)} %slice.647), channel_id=1, source_target_pairs={{0,32},{32,64},{64,96},{96,128},{128,160},{160,192},{192,224},{224... | collective-permute-start | bytes 12296 | tf_op jit(solution)/shard_map/ppermute | solution.py:38
  78.9 9.4 %collective-permute-start.16 = (f32[8,1,128]{2,1,0:T(1,128)S(1)}, f32[8,1,128]{2,1,0:T(1,128)S(1)}, u32[]{:S(2)}, u32[]{:S(2)}) collective-permute-start(f32[8,1,128]{2,1,0:T(1,128)S(1)} %slice.663), channel_id=1, source_target_pairs={{32,0},{64,32},{96,64},{128,96},{160,128},{192,160},{224,192},{256... | collective-permute-start | bytes 12296 | tf_op jit(solution)/shard_map/ppermute | solution.py:38
  88.6 12.5 %collective-permute-start.18 = (f32[8,16,1]{2,1,0:T(8,128)S(1)}, f32[8,16,1]{2,1,0:T(8,128)S(1)}, u32[]{:S(2)}, u32[]{:S(2)}) collective-permute-start(f32[8,16,1]{2,1,0:T(8,128)S(1)} %slice.667), channel_id=1, source_target_pairs={{0,2},{2,4},{4,6},{6,8},{8,10},{10,12},{12,14},{14,16},{16,18},{18... | collective-permute-start | bytes 1544 | tf_op jit(solution)/shard_map/ppermute | solution.py:38
  93.8 10.3 %collective-permute-start.21 = (f32[8,1,128]{2,1,0:T(1,128)S(1)}, f32[8,1,128]{2,1,0:T(1,128)S(1)}, u32[]{:S(2)}, u32[]{:S(2)}) collective-permute-start(f32[8,1,128]{2,1,0:T(1,128)S(1)} %slice.675), channel_id=1, source_target_pairs={{0,32},{32,64},{64,96},{96,128},{128,160},{160,192},{192,224},{224... | collective-permute-start | bytes 12296 | tf_op jit(solution)/shard_map/ppermute | solution.py:38
  108.9 10.3 %collective-permute-start.22 = (f32[8,1,128]{2,1,0:T(1,128)S(1)}, f32[8,1,128]{2,1,0:T(1,128)S(1)}, u32[]{:S(2)}, u32[]{:S(2)}) collective-permute-start(f32[8,1,128]{2,1,0:T(1,128)S(1)} %slice.677), channel_id=1, source_target_pairs={{0,32},{32,64},{64,96},{96,128},{128,160},{160,192},{192,224},{224... | collective-permute-start | bytes 12296 | tf_op jit(solution)/shard_map/ppermute | solution.py:38
  131.7 9.5 %collective-permute-start.28 = (f32[8,1,128]{2,1,0:T(1,128)S(1)}, f32[8,1,128]{2,1,0:T(1,128)S(1)}, u32[]{:S(2)}, u32[]{:S(2)}) collective-permute-start(f32[8,1,128]{2,1,0:T(1,128)S(1)} %slice.693), channel_id=1, source_target_pairs={{32,0},{64,32},{96,64},{128,96},{160,128},{192,160},{224,192},{256... | collective-permute-start | bytes 12296 | tf_op jit(solution)/shard_map/ppermute | solution.py:38
  141.6 12.4 %collective-permute-start.30 = (f32[8,16,1]{2,1,0:T(8,128)S(1)}, f32[8,16,1]{2,1,0:T(8,128)S(1)}, u32[]{:S(2)}, u32[]{:S(2)}) collective-permute-start(f32[8,16,1]{2,1,0:T(8,128)S(1)} %slice.697), channel_id=1, source_target_pairs={{0,2},{2,4},{4,6},{6,8},{8,10},{10,12},{12,14},{14,16},{16,18},{18... | collective-permute-start | bytes 1544 | tf_op jit(solution)/shard_map/ppermute | solution.py:38
  146.7 10.3 %collective-permute-start.33 = (f32[8,1,128]{2,1,0:T(1,128)S(1)}, f32[8,1,128]{2,1,0:T(1,128)S(1)}, u32[]{:S(2)}, u32[]{:S(2)}) collective-permute-start(f32[8,1,128]{2,1,0:T(1,128)S(1)} %slice.705), channel_id=1, source_target_pairs={{0,32},{32,64},{64,96},{96,128},{128,160},{160,192},{192,224},{224... | collective-permute-start | bytes 12296 | tf_op jit(solution)/shard_map/ppermute | solution.py:38
  157.2 10.5 %collective-permute-start.35 = (f32[8,16,1]{2,1,0:T(8,128)S(1)}, f32[8,16,1]{2,1,0:T(8,128)S(1)}, u32[]{:S(2)}, u32[]{:S(2)}) collective-permute-start(f32[8,16,1]{2,1,0:T(8,128)S(1)} %slice.709), channel_id=1, source_target_pairs={{0,2},{2,4},{4,6},{6,8},{8,10},{10,12},{12,14},{14,16},{16,18},{18... | collective-permute-start | bytes 1544 | tf_op jit(solution)/shard_map/ppermute | solution.py:38
  163.8 10.3 %collective-permute-start.34 = (f32[8,1,128]{2,1,0:T(1,128)S(1)}, f32[8,1,128]{2,1,0:T(1,128)S(1)}, u32[]{:S(2)}, u32[]{:S(2)}) collective-permute-start(f32[8,1,128]{2,1,0:T(1,128)S(1)} %slice.707), channel_id=1, source_target_pairs={{0,32},{32,64},{64,96},{96,128},{128,160},{160,192},{192,224},{224... | collective-permute-start | bytes 12296 | tf_op jit(solution)/shard_map/ppermute | solution.py:38
  186.7 9.5 %collective-permute-start.40 = (f32[8,1,128]{2,1,0:T(1,128)S(1)}, f32[8,1,128]{2,1,0:T(1,128)S(1)}, u32[]{:S(2)}, u32[]{:S(2)}) collective-permute-start(f32[8,1,128]{2,1,0:T(1,128)S(1)} %slice.723), channel_id=1, source_target_pairs={{32,0},{64,32},{96,64},{128,96},{160,128},{192,160},{224,192},{256... | collective-permute-start | bytes 12296 | tf_op jit(solution)/shard_map/ppermute | solution.py:38
  196.6 12.4 %collective-permute-start.42 = (f32[8,16,1]{2,1,0:T(8,128)S(1)}, f32[8,16,1]{2,1,0:T(8,128)S(1)}, u32[]{:S(2)}, u32[]{:S(2)}) collective-permute-start(f32[8,16,1]{2,1,0:T(8,128)S(1)} %slice.727), channel_id=1, source_target_pairs={{0,2},{2,4},{4,6},{6,8},{8,10},{10,12},{12,14},{14,16},{16,18},{18... | collective-permute-start | bytes 1544 | tf_op jit(solution)/shard_map/ppermute | solution.py:38
  201.7 10.3 %collective-permute-start.45 = (f32[8,1,128]{2,1,0:T(1,128)S(1)}, f32[8,1,128]{2,1,0:T(1,128)S(1)}, u32[]{:S(2)}, u32[]{:S(2)}) collective-permute-start(f32[8,1,128]{2,1,0:T(1,128)S(1)} %slice.735), channel_id=1, source_target_pairs={{0,32},{32,64},{64,96},{96,128},{128,160},{160,192},{192,224},{224... | collective-permute-start | bytes 12296 | tf_op jit(solution)/shard_map/ppermute | solution.py:38
  212.2 10.5 %collective-permute-start.47 = (f32[8,16,1]{2,1,0:T(8,128)S(1)}, f32[8,16,1]{2,1,0:T(8,128)S(1)}, u32[]{:S(2)}, u32[]{:S(2)}) collective-permute-start(f32[8,16,1]{2,1,0:T(8,128)S(1)} %slice.739), channel_id=1, source_target_pairs={{0,2},{2,4},{4,6},{6,8},{8,10},{10,12},{12,14},{14,16},{16,18},{18... | collective-permute-start | bytes 1544 | tf_op jit(solution)/shard_map/ppermute | solution.py:38
  218.8 10.3 %collective-permute-start.46 = (f32[8,1,128]{2,1,0:T(1,128)S(1)}, f32[8,1,128]{2,1,0:T(1,128)S(1)}, u32[]{:S(2)}, u32[]{:S(2)}) collective-permute-start(f32[8,1,128]{2,1,0:T(1,128)S(1)} %slice.737), channel_id=1, source_target_pairs={{0,32},{32,64},{64,96},{96,128},{128,160},{160,192},{192,224},{224... | collective-permute-start | bytes 12296 | tf_op jit(solution)/shard_map/ppermute | solution.py:38
  231.6 236.9 %all-reduce.3.cloned.1.call-start = ((), (), s32[]{:S(2)}) async-start(), calls=%async_computation.2 | async-start | bytes 1048576 | tf_op jit(solution)/shard_map/psum | solution.py:170
  261.3 379.4 %all-reduce.5.cloned.1.call-start = ((), (), s32[]{:S(2)}) async-start(), calls=%async_computation.3 | async-start | bytes 1048576 | tf_op jit(solution)/shard_map/psum | solution.py:170
  (34 other events, 241.3 us)
Sparse Core Ops, SparseCore 0:
  231.8 16.1 reduce-scatter.1
  261.5 207.0 all-reduce.2
  471.4 169.2 all-reduce.4
